TPU v7x, 512 devices: a whole 4x8x8 slice. The times are simulated.
512 devices in a mesh: gx: 64 (over y_hi, z, core), gy: 8 (over x, y_lo).
Axes of the slice: x: 4, y: 8 (y_hi: 4, y_lo: 2; y = y_hi * 2 + y_lo), z: 8, core: 2. Of those that a mesh axis runs over, the one named last changes fastest.
Arguments:
- fwd_pops: bfloat16 [3, 19, 256, 64, 128], P(None, None, 'gx', 'gy'), may hold values from -4 to 4
- fwd_scale: float32 [3, 256, 64, 128], P(None, 'gx', 'gy'), may hold values from 0.01 to 0.1
- seed_adjoint: float32 [19, 256, 64, 128], P(None, 'gx', 'gy'), may hold values from -16 to 16
- turbine_map: int32 [256, 64, 128], P('gx', 'gy'), may hold values from -1 to 39, as said below
- thrust: float32 [40], replicated, may hold values from 0.4 to 0.88
Outputs:
- adjoint_out: float32 [19, 256, 64, 128], P(None, 'gx', 'gy')
- thrust_grad: float32 [40], replicated
Inputs may be any that keep to these rules, and one draw needn't show every extreme that they name: `turbine_map`: every turbine's disk is the set of cells in one streamwise plane within 4 cells (Euclidean, spanwise distance wrapping) of its centre; disks never intersect and every turbine covers cells.
All inputs are finite; a program needn't handle non-finite values.
Results may differ from a plain program's by a relative error of at most 0.0003.
Values sent between devices are 32-bit elements; how exact they have to be, the bound alone decides.
A program may use at most 64 MiB of HBM per device.

v0:
```python
import jax
import jax.numpy as jnp
from jax import lax
from jax.sharding import PartitionSpec as P

VELOCITIES = (
    (0, 0, 0),
    (1, 0, 0),
    (-1, 0, 0),
    (0, 1, 0),
    (0, -1, 0),
    (0, 0, 1),
    (0, 0, -1),
    (1, 1, 0),
    (-1, -1, 0),
    (1, -1, 0),
    (-1, 1, 0),
    (1, 0, 1),
    (-1, 0, -1),
    (1, 0, -1),
    (-1, 0, 1),
    (0, 1, 1),
    (0, -1, -1),
    (0, 1, -1),
    (0, -1, 1),
)
OPPOSITE = (0, 2, 1, 4, 3, 6, 5, 8, 7, 10, 9, 12, 11, 14, 13, 16, 15, 18, 17)
WEIGHTS = tuple([1.0 / 3.0] + [1.0 / 18.0] * 6 + [1.0 / 36.0] * 12)
MEAN_FLOW = 0.1
TAU_BASE = 0.51
SMAG_COEF = 18.0 * 1.4142135623730951 * 0.17 * 0.17
QUAD_FLOOR = 0.0001
PAIRS = ((0, 0, 1.0), (1, 1, 1.0), (2, 2, 1.0), (0, 1, 2.0), (0, 2, 2.0), (1, 2, 2.0))


def extended(block, sides, width):
    for axis, dim in sides:
        count = lax.axis_size(axis)
        forward = [(i, i + 1) for i in range(count - 1)]
        forward.append((count - 1, 0))
        backward = [(target, source) for source, target in forward]
        low = lax.ppermute(
            lax.slice_in_dim(block, block.shape[dim] - width, None, axis=dim), axis, forward
        )
        high = lax.ppermute(lax.slice_in_dim(block, 0, width, axis=dim), axis, backward)
        block = jnp.concatenate([low, block, high], axis=dim)
    return block


def base_values():
    values = []
    for member in range(19):
        along = float(VELOCITIES[member][0])
        values.append(
            WEIGHTS[member]
            * (
                1.0
                + 3.0 * MEAN_FLOW * along
                + 4.5 * MEAN_FLOW * MEAN_FLOW * along * along
                - 1.5 * MEAN_FLOW * MEAN_FLOW
            )
        )
    return values


def decode(stored, scaling):
    base = jnp.asarray(base_values(), dtype=jnp.float32)
    return base[:, None, None, None] * (1.0 + scaling[None] * stored.astype(jnp.float32))


def collide(populations, thrust_cell):
    density = populations[0]
    for member in range(1, 19):
        density = density + populations[member]
    velocity = []
    for axis_id in range(3):
        moment = jnp.zeros_like(density)
        for member in range(19):
            component = VELOCITIES[member][axis_id]
            if component != 0:
                moment = moment + float(component) * populations[member]
        velocity.append(moment / density)
    speed_sq = velocity[0] * velocity[0] + velocity[1] * velocity[1] + velocity[2] * velocity[2]
    nonequil = []
    for member in range(19):
        proj = (
            float(VELOCITIES[member][0]) * velocity[0]
            + float(VELOCITIES[member][1]) * velocity[1]
            + float(VELOCITIES[member][2]) * velocity[2]
        )
        equilib = (
            WEIGHTS[member] * density * (1.0 + 3.0 * proj + 4.5 * proj * proj - 1.5 * speed_sq)
        )
        nonequil.append(populations[member] - equilib)
    stress_sum = jnp.zeros_like(density)
    for first, second, factor in PAIRS:
        stress = jnp.zeros_like(density)
        for member in range(19):
            product = VELOCITIES[member][first] * VELOCITIES[member][second]
            if product != 0:
                stress = stress + float(product) * nonequil[member]
        stress_sum = stress_sum + factor * stress * stress
    magnitude = jnp.sqrt(stress_sum + QUAD_FLOOR)
    relaxation = 0.5 * (TAU_BASE + jnp.sqrt(TAU_BASE * TAU_BASE + SMAG_COEF * magnitude / density))
    thrust_force = -0.5 * thrust_cell * velocity[0] * jnp.abs(velocity[0])
    result = []
    for member in range(19):
        result.append(
            populations[member]
            - nonequil[member] / relaxation
            + 3.0 * WEIGHTS[member] * float(VELOCITIES[member][0]) * thrust_force
        )
    return jnp.stack(result)


def local_thrust(values):
    return 4.0 * values / jnp.square(1.0 + jnp.sqrt(1.0 - values))


def finish_vertical(shifted, adjoint):
    result = []
    for member in range(19):
        vertical = VELOCITIES[member][2]
        mirror = adjoint[OPPOSITE[member]]
        if vertical == 1:
            result.append(jnp.concatenate([shifted[member][..., 1:], mirror[..., -1:]], axis=-1))
        elif vertical == -1:
            result.append(jnp.concatenate([mirror[..., :1], shifted[member][..., :-1]], axis=-1))
        else:
            result.append(shifted[member])
    return jnp.stack(result)


def pull_whole(adjoint):
    width_x = adjoint.shape[1]
    width_y = adjoint.shape[2]
    padded = extended(adjoint, (("gx", 1), ("gy", 2)), 1)
    shifted = []
    for member in range(19):
        start_x = 1 + VELOCITIES[member][0]
        start_y = 1 + VELOCITIES[member][1]
        shifted.append(padded[member, start_x : start_x + width_x, start_y : start_y + width_y])
    return shifted


def shards(fwd_pops, fwd_scale, seed_adjoint, turbine_map, thrust):
    steps_count = fwd_pops.shape[0]
    turbines = thrust.shape[0]
    inside = turbine_map >= 0
    ids = jnp.maximum(turbine_map, 0)
    thrust_cell = jnp.where(inside, jnp.take(local_thrust(thrust), ids), 0.0)
    selector = (
        turbine_map.reshape(-1)[None, :] == jnp.arange(turbines, dtype=jnp.int32)[:, None]
    ).astype(jnp.float32)
    adjoint = seed_adjoint
    summed = jnp.zeros((turbines,), jnp.float32)
    for instant in range(steps_count - 1, -1, -1):
        shifted = pull_whole(adjoint)
        incoming = finish_vertical(shifted, adjoint)
        populations = decode(fwd_pops[instant], fwd_scale[instant])
        _, pullback = jax.vjp(collide, populations, thrust_cell)
        adjoint, cell_grad = pullback(incoming)
        partial_value = jnp.dot(selector, cell_grad.reshape(-1), precision=lax.Precision.HIGHEST)
        summed = summed + lax.psum(partial_value, ("gx", "gy"))
    _, slope = jax.vjp(local_thrust, thrust)
    thrust_grad = slope(summed)[0]
    return (adjoint, thrust_grad)


def solution(mesh):
    placed = (
        P(None, None, "gx", "gy", None),
        P(None, "gx", "gy", None),
        P(None, "gx", "gy", None),
        P("gx", "gy", None),
        P(),
    )
    return jax.shard_map(
        shards,
        mesh=mesh,
        in_specs=placed,
        out_specs=(P(None, "gx", "gy", None), P()),
        check_vma=False,
    )
```

profile of v0, /device:TPU:1, one launch (start us, length us, event | category | flops | bytes accessed | tf_op | source)
XLA Modules:
  0.0 210.3 jit_solution(3809331997882569221)
XLA Ops:
  0.6 1.0 fusion.1098
  1.6 5.4 %collective-permute-start = (f32[19,1,8,128]{3,2,1,0:T(8,128)S(1)}, f32[19,1,8,128]{3,2,1,0:T(8,128)S(1)}, u32[]{:S(2)}, u32[]{:S(2)}) collective-permute-start(f32[19,1,8,128]{3,2,1,0:T(8,128)S(1)} %get-tuple-element.324), channel_id=1, source_target_pairs={{0,8},{8,16},{16,24},{24,32},{32,40},{40,48},{48,56},{56,64},{64,7... | collective-permute-start | bytes 233480 | tf_op jit(solution)/shard_map/ppermute | solution.py:42
  7.0 5.4 %collective-permute-start.1 = (f32[19,1,8,128]{3,2,1,0:T(8,128)S(1)}, f32[19,1,8,128]{3,2,1,0:T(8,128)S(1)}, u32[]{:S(2)}, u32[]{:S(2)}) collective-permute-start(f32[19,1,8,128]{3,2,1,0:T(8,128)S(1)} %get-tuple-element.325), channel_id=1, source_target_pairs={{8,0},{16,8},{24,16},{32,24},{40,32},{48,40},{56,48},{64,56},{72,6... | collective-permute-start | bytes 233480 | tf_op jit(solution)/shard_map/ppermute | solution.py:45
  12.6 0.6 copy-done.2
  13.7 0.7 copy-done.5
  14.5 0.5 copy-done.6
  15.0 24.7 %gather_fusion = f32[4096]{0:T(1024)S(1)} fusion(f32[40]{0:T(128)S(1)} %multiply_divide_fusion, s32[4096]{0:T(1024)S(1)} %bitcast_clamp_fusion), kind=kCustom, calls=%fused_computation | custom fusion | bytes 49152 | tf_op jit(solution)/shard_map/jit(_take)/gather | solution.py:151
  40.0 2.0 collective-permute-start.3
  42.0 3.3 %collective-permute-start.2 = (f32[19,6,1,128]{3,2,1,0:T(1,128)S(1)}, f32[19,6,1,128]{3,2,1,0:T(1,128)S(1)}, u32[]{:S(2)}, u32[]{:S(2)}) collective-permute-start(f32[19,6,1,128]{3,2,1,0:T(1,128)S(1)} %get-tuple-element.262), channel_id=1, source_target_pairs={{0,1},{1,2},{2,3},{3,4},{4,5},{5,6},{6,7},{7,0},{8,9},{9,10},{10,1... | collective-permute-start | bytes 175112 | tf_op jit(solution)/shard_map/ppermute | solution.py:42
  45.4 3.6 %collective-permute-done.2 = f32[19,6,1,128]{3,2,1,0:T(1,128)S(1)} collective-permute-done((f32[19,6,1,128]{3,2,1,0:T(1,128)S(1)}, f32[19,6,1,128]{3,2,1,0:T(1,128)S(1)}, u32[]{:S(2)}, u32[]{:S(2)}) %collective-permute-start.2) | collective-permute-done | bytes 58400 | tf_op jit(solution)/shard_map/ppermute | solution.py:42
  49.3 0.3 fusion.127
  49.8 0.4 broadcast_multiply_fusion.11
  50.2 0.3 divide_multiply_fusion.4
  50.5 0.3 multiply_bitcast_fusion.2
  50.8 0.5 fusion.670
  51.4 0.2 broadcast_multiply_fusion.10
  51.5 0.6 copy-done.4
  52.3 5.2 %collective-permute-start.4 = (f32[19,1,8,128]{3,2,1,0:T(8,128)S(1)}, f32[19,1,8,128]{3,2,1,0:T(8,128)S(1)}, u32[]{:S(2)}, u32[]{:S(2)}) collective-permute-start(f32[19,1,8,128]{3,2,1,0:T(8,128)S(1)} %get-tuple-element.309), channel_id=1, source_target_pairs={{0,8},{8,16},{16,24},{24,32},{32,40},{40,48},{48,56},{56,64},{64,7... | collective-permute-start | bytes 233480 | tf_op jit(solution)/shard_map/ppermute | solution.py:42
  57.6 9.4 %collective-permute-start.5 = (f32[19,1,8,128]{3,2,1,0:T(8,128)S(1)}, f32[19,1,8,128]{3,2,1,0:T(8,128)S(1)}, u32[]{:S(2)}, u32[]{:S(2)}) collective-permute-start(f32[19,1,8,128]{3,2,1,0:T(8,128)S(1)} %get-tuple-element.310), channel_id=1, source_target_pairs={{8,0},{16,8},{24,16},{32,24},{40,32},{48,40},{56,48},{64,56},{72,6... | collective-permute-start | bytes 233480 | tf_op jit(solution)/shard_map/ppermute | solution.py:45
  66.9 0.4 convolution_bitcast_fusion.2
  67.3 0.5 collective-permute-done.5
  68.1 1.9 collective-permute-start.7
  70.0 3.4 %collective-permute-start.6 = (f32[19,6,1,128]{3,2,1,0:T(1,128)S(1)}, f32[19,6,1,128]{3,2,1,0:T(1,128)S(1)}, u32[]{:S(2)}, u32[]{:S(2)}) collective-permute-start(f32[19,6,1,128]{3,2,1,0:T(1,128)S(1)} %get-tuple-element.258), channel_id=1, source_target_pairs={{0,1},{1,2},{2,3},{3,4},{4,5},{5,6},{6,7},{7,0},{8,9},{9,10},{10,1... | collective-permute-start | bytes 175112 | tf_op jit(solution)/shard_map/ppermute | solution.py:42
  73.9 3.2 %collective-permute-done.6 = f32[19,6,1,128]{3,2,1,0:T(1,128)S(1)} collective-permute-done((f32[19,6,1,128]{3,2,1,0:T(1,128)S(1)}, f32[19,6,1,128]{3,2,1,0:T(1,128)S(1)}, u32[]{:S(2)}, u32[]{:S(2)}) %collective-permute-start.6) | collective-permute-done | bytes 58400 | tf_op jit(solution)/shard_map/ppermute | solution.py:42
  77.4 0.3 add_add_fusion.54
  77.8 0.3 broadcast_multiply_fusion.13
  78.2 0.3 divide_multiply_fusion.2
  78.5 0.3 multiply_bitcast_fusion.1
  78.8 0.5 fusion.682
  79.3 0.2 broadcast_multiply_fusion.12
  79.5 0.5 pad_add_fusion.1
  80.0 1.9 collective-permute-start.8
  82.0 10.1 %collective-permute-start.9 = (f32[19,1,8,128]{3,2,1,0:T(8,128)S(1)}, f32[19,1,8,128]{3,2,1,0:T(8,128)S(1)}, u32[]{:S(2)}, u32[]{:S(2)}) collective-permute-start(f32[19,1,8,128]{3,2,1,0:T(8,128)S(1)} %get-tuple-element.296), channel_id=1, source_target_pairs={{8,0},{16,8},{24,16},{32,24},{40,32},{48,40},{56,48},{64,56},{72,6... | collective-permute-start | bytes 233480 | tf_op jit(solution)/shard_map/ppermute | solution.py:45
  92.1 0.4 fusion.1
  92.5 0.5 collective-permute-done.9
  93.3 1.9 collective-permute-start.11
  95.2 3.4 %collective-permute-start.10 = (f32[19,6,1,128]{3,2,1,0:T(1,128)S(1)}, f32[19,6,1,128]{3,2,1,0:T(1,128)S(1)}, u32[]{:S(2)}, u32[]{:S(2)}) collective-permute-start(f32[19,6,1,128]{3,2,1,0:T(1,128)S(1)} %get-tuple-element.254), channel_id=1, source_target_pairs={{0,1},{1,2},{2,3},{3,4},{4,5},{5,6},{6,7},{7,0},{8,9},{9,10},{10,1... | collective-permute-start | bytes 175112 | tf_op jit(solution)/shard_map/ppermute | solution.py:42
  99.0 3.2 %collective-permute-done.10 = f32[19,6,1,128]{3,2,1,0:T(1,128)S(1)} collective-permute-done((f32[19,6,1,128]{3,2,1,0:T(1,128)S(1)}, f32[19,6,1,128]{3,2,1,0:T(1,128)S(1)}, u32[]{:S(2)}, u32[]{:S(2)}) %collective-permute-start.10) | collective-permute-done | bytes 58400 | tf_op jit(solution)/shard_map/ppermute | solution.py:42
  102.5 0.4 fusion
  103.0 103.2 %psum.25 = f32[40]{0:T(128)S(1)} all-reduce(f32[40]{0:T(128)S(1)} %fusion), channel_id=1, replica_groups=mesh['gx'=64,'gy'=8] {'gx','gy'}, use_global_device_ids=true, to_apply=%region_0.1 | all-reduce | flops 40 | bytes 320 | tf_op jit(solution)/shard_map/psum | solution.py:164
  206.2 0.5 multiply_add_fusion.114
  206.8 0.3 add_add_fusion.26
  207.2 0.3 broadcast_multiply_fusion.9
  207.5 0.3 divide_multiply_fusion
  207.9 0.3 multiply_bitcast_fusion
  208.2 0.5 fusion.694
  208.7 0.2 broadcast_multiply_fusion.14
  208.9 1.4 pad_add_fusion
  (98 shorter events, 3.8 us)
Async XLA Ops:
  0.6 11.8 %copy-start = (f32[19,4,8,128]{3,2,1,0:T(8,128)S(1)}, f32[19,4,8,128]{3,2,1,0:T(8,128)}, u32[]{:S(2)}) copy-start(f32[19,4,8,128]{3,2,1,0:T(8,128)} %param.10) | copy-start | bytes 933892
  1.6 38.1 %collective-permute-start = (f32[19,1,8,128]{3,2,1,0:T(8,128)S(1)}, f32[19,1,8,128]{3,2,1,0:T(8,128)S(1)}, u32[]{:S(2)}, u32[]{:S(2)}) collective-permute-start(f32[19,1,8,128]{3,2,1,0:T(8,128)S(1)} %get-tuple-element.324), channel_id=1, source_target_pairs={{0,8},{8,16},{16,24},{24,32},{32,40},{40,48},{48,56},{56,64},{64,7... | collective-permute-start | bytes 233480 | tf_op jit(solution)/shard_map/ppermute | solution.py:42
  7.0 6.7 %copy-start.1 = (bf16[3,19,4,8,128]{4,3,2,1,0:T(8,128)(2,1)S(1)}, bf16[3,19,4,8,128]{4,3,2,1,0:T(8,128)(2,1)}, u32[]{:S(2)}) copy-start(bf16[3,19,4,8,128]{4,3,2,1,0:T(8,128)(2,1)} %param.8) | copy-start | bytes 1400836
  7.0 32.8 %collective-permute-start.1 = (f32[19,1,8,128]{3,2,1,0:T(8,128)S(1)}, f32[19,1,8,128]{3,2,1,0:T(8,128)S(1)}, u32[]{:S(2)}, u32[]{:S(2)}) collective-permute-start(f32[19,1,8,128]{3,2,1,0:T(8,128)S(1)} %get-tuple-element.325), channel_id=1, source_target_pairs={{8,0},{16,8},{24,16},{32,24},{40,32},{48,40},{56,48},{64,56},{72,6... | collective-permute-start | bytes 233480 | tf_op jit(solution)/shard_map/ppermute | solution.py:45
  12.6 0.7 copy-start.2
  12.6 0.8 copy-start.3
  13.7 0.7 copy-start.5
  14.3 0.7 copy-start.6
  40.0 5.4 %collective-permute-start.3 = (f32[19,6,1,128]{3,2,1,0:T(1,128)S(1)}, f32[19,6,1,128]{3,2,1,0:T(1,128)S(1)}, u32[]{:S(2)}, u32[]{:S(2)}) collective-permute-start(f32[19,6,1,128]{3,2,1,0:T(1,128)S(1)} %get-tuple-element.261), channel_id=1, source_target_pairs={{1,0},{2,1},{3,2},{4,3},{5,4},{6,5},{7,6},{0,7},{9,8},{10,9},{11,1... | collective-permute-start | bytes 175112 | tf_op jit(solution)/shard_map/ppermute | solution.py:45
  42.0 7.0 %collective-permute-start.2 = (f32[19,6,1,128]{3,2,1,0:T(1,128)S(1)}, f32[19,6,1,128]{3,2,1,0:T(1,128)S(1)}, u32[]{:S(2)}, u32[]{:S(2)}) collective-permute-start(f32[19,6,1,128]{3,2,1,0:T(1,128)S(1)} %get-tuple-element.262), channel_id=1, source_target_pairs={{0,1},{1,2},{2,3},{3,4},{4,5},{5,6},{6,7},{7,0},{8,9},{9,10},{10,1... | collective-permute-start | bytes 175112 | tf_op jit(solution)/shard_map/ppermute | solution.py:42
  51.5 0.7 copy-start.4
  52.3 15.0 %collective-permute-start.4 = (f32[19,1,8,128]{3,2,1,0:T(8,128)S(1)}, f32[19,1,8,128]{3,2,1,0:T(8,128)S(1)}, u32[]{:S(2)}, u32[]{:S(2)}) collective-permute-start(f32[19,1,8,128]{3,2,1,0:T(8,128)S(1)} %get-tuple-element.309), channel_id=1, source_target_pairs={{0,8},{8,16},{16,24},{24,32},{32,40},{40,48},{48,56},{56,64},{64,7... | collective-permute-start | bytes 233480 | tf_op jit(solution)/shard_map/ppermute | solution.py:42
  57.6 10.3 %collective-permute-start.5 = (f32[19,1,8,128]{3,2,1,0:T(8,128)S(1)}, f32[19,1,8,128]{3,2,1,0:T(8,128)S(1)}, u32[]{:S(2)}, u32[]{:S(2)}) collective-permute-start(f32[19,1,8,128]{3,2,1,0:T(8,128)S(1)} %get-tuple-element.310), channel_id=1, source_target_pairs={{8,0},{16,8},{24,16},{32,24},{40,32},{48,40},{56,48},{64,56},{72,6... | collective-permute-start | bytes 233480 | tf_op jit(solution)/shard_map/ppermute | solution.py:45
  68.1 5.8 %collective-permute-start.7 = (f32[19,6,1,128]{3,2,1,0:T(1,128)S(1)}, f32[19,6,1,128]{3,2,1,0:T(1,128)S(1)}, u32[]{:S(2)}, u32[]{:S(2)}) collective-permute-start(f32[19,6,1,128]{3,2,1,0:T(1,128)S(1)} %get-tuple-element.257), channel_id=1, source_target_pairs={{1,0},{2,1},{3,2},{4,3},{5,4},{6,5},{7,6},{0,7},{9,8},{10,9},{11,1... | collective-permute-start | bytes 175112 | tf_op jit(solution)/shard_map/ppermute | solution.py:45
  70.0 7.0 %collective-permute-start.6 = (f32[19,6,1,128]{3,2,1,0:T(1,128)S(1)}, f32[19,6,1,128]{3,2,1,0:T(1,128)S(1)}, u32[]{:S(2)}, u32[]{:S(2)}) collective-permute-start(f32[19,6,1,128]{3,2,1,0:T(1,128)S(1)} %get-tuple-element.258), channel_id=1, source_target_pairs={{0,1},{1,2},{2,3},{3,4},{4,5},{5,6},{6,7},{7,0},{8,9},{9,10},{10,1... | collective-permute-start | bytes 175112 | tf_op jit(solution)/shard_map/ppermute | solution.py:42
  80.0 12.5 %collective-permute-start.8 = (f32[19,1,8,128]{3,2,1,0:T(8,128)S(1)}, f32[19,1,8,128]{3,2,1,0:T(8,128)S(1)}, u32[]{:S(2)}, u32[]{:S(2)}) collective-permute-start(f32[19,1,8,128]{3,2,1,0:T(8,128)S(1)} %get-tuple-element.295), channel_id=1, source_target_pairs={{0,8},{8,16},{16,24},{24,32},{32,40},{40,48},{48,56},{56,64},{64,7... | collective-permute-start | bytes 233480 | tf_op jit(solution)/shard_map/ppermute | solution.py:42
  82.0 11.0 %collective-permute-start.9 = (f32[19,1,8,128]{3,2,1,0:T(8,128)S(1)}, f32[19,1,8,128]{3,2,1,0:T(8,128)S(1)}, u32[]{:S(2)}, u32[]{:S(2)}) collective-permute-start(f32[19,1,8,128]{3,2,1,0:T(8,128)S(1)} %get-tuple-element.296), channel_id=1, source_target_pairs={{8,0},{16,8},{24,16},{32,24},{40,32},{48,40},{56,48},{64,56},{72,6... | collective-permute-start | bytes 233480 | tf_op jit(solution)/shard_map/ppermute | solution.py:45
  93.3 5.8 %collective-permute-start.11 = (f32[19,6,1,128]{3,2,1,0:T(1,128)S(1)}, f32[19,6,1,128]{3,2,1,0:T(1,128)S(1)}, u32[]{:S(2)}, u32[]{:S(2)}) collective-permute-start(f32[19,6,1,128]{3,2,1,0:T(1,128)S(1)} %get-tuple-element.253), channel_id=1, source_target_pairs={{1,0},{2,1},{3,2},{4,3},{5,4},{6,5},{7,6},{0,7},{9,8},{10,9},{11,1... | collective-permute-start | bytes 175112 | tf_op jit(solution)/shard_map/ppermute | solution.py:45
  95.2 7.0 %collective-permute-start.10 = (f32[19,6,1,128]{3,2,1,0:T(1,128)S(1)}, f32[19,6,1,128]{3,2,1,0:T(1,128)S(1)}, u32[]{:S(2)}, u32[]{:S(2)}) collective-permute-start(f32[19,6,1,128]{3,2,1,0:T(1,128)S(1)} %get-tuple-element.254), channel_id=1, source_target_pairs={{0,1},{1,2},{2,3},{3,4},{4,5},{5,6},{6,7},{7,0},{8,9},{9,10},{10,1... | collective-permute-start | bytes 175112 | tf_op jit(solution)/shard_map/ppermute | solution.py:42
where the time goes:
time: 211 us; the launch traced here: 210 us
  blocking collectives  103 us (49%)
  starting transfers between devices  53.2 us (25%)
  local copies, waits for them, and re-layouts  30.7 us (15%)
  waiting for transfers between devices  11 us (5%)
  other arithmetic  9.76 us (5%)
    psum x1, blocking collectives, shards(): summed = summed + lax.psum(partial_value, ('gx', 'gy'))  103 us
    ppermute x6, starting transfers between devices, extended(): lax.ppermute(lax.slice_in_dim(block, 0, width, axis=dim), axis, backward)  30.8 us
    gather x1, local copies, waits for them, and re-layouts, shards(): thrust_cell = jnp.where(inside, jnp.take(local_thrust(thrust), ids), 0.0)  24.7 us
    ppermute x6, starting transfers between devices, extended(): lax.ppermute(lax.slice_in_dim(block, block.shape[dim] - width, None, axis...  22.5 us
    ppermute x6, waiting for transfers between devices, extended(): lax.ppermute(lax.slice_in_dim(block, block.shape[dim] - width, None, axis...  9.99 us
  transfers between devices with their start and end apart: 12, of which 5 were waited for; matrix products, arithmetic and copies ran while one was open for 13% of the time, Pallas kernels for 0%

commit v1 on v0

--- a/solution.py
+++ b/solution.py
@@ -161,7 +161,7 @@
         _, pullback = jax.vjp(collide, populations, thrust_cell)
         adjoint, cell_grad = pullback(incoming)
         partial_value = jnp.dot(selector, cell_grad.reshape(-1), precision=lax.Precision.HIGHEST)
-        summed = summed + lax.psum(partial_value, ("gx", "gy"))
+        summed = summed + jnp.sum(lax.all_gather(partial_value, ("gx", "gy")), axis=0)
     _, slope = jax.vjp(local_thrust, thrust)
     thrust_grad = slope(summed)[0]
     return (adjoint, thrust_grad)

time: 211 us -> 395 us (1.87)
  waiting for transfers between devices: 11 us -> 275 us
  blocking collectives: 103 us -> 0 us
  between operations: 1.09 us -> 14.6 us
  local copies, waits for them, and re-layouts: 30.7 us -> 35.9 us
  starting transfers between devices: 53.2 us -> 57.5 us
    unnamed x0 -> x2, waiting for transfers between devices: none -> 273 us
    psum x1 -> x0, blocking collectives: 103 us -> none  [shards(): summed = summed + lax.psum(partial_value, ('gx', 'gy'))]
    ppermute x6, waiting for transfers between devices: 9.99 us -> 0.02 us  [extended(): lax.ppermute(lax.slice_in_dim(block, block.shape[dim] - width, None, axis...]
    ppermute x6, starting transfers between devices: 30.8 us -> 40.2 us  [extended(): lax.ppermute(lax.slice_in_dim(block, 0, width, axis=dim), axis, backward)]
    ppermute x6, starting transfers between devices: 22.5 us -> 17.4 us  [extended(): lax.ppermute(lax.slice_in_dim(block, block.shape[dim] - width, None, axis...]
  transfers between devices with their start and end apart: 12 -> 13, of which waited for: 5 -> 6; matrix products, arithmetic and copies ran while one was open for 13% -> 8% of each run, Pallas kernels for 0% -> 0%
where the time goes in v1:
time: 395 us
  waiting for transfers between devices  275 us (70%)
  starting transfers between devices  57.5 us (15%)
  local copies, waits for them, and re-layouts  35.9 us (9%)
  between operations  14.6 us (4%)
  other arithmetic  10.1 us (3%)
    unnamed x2, waiting for transfers between devices  273 us
    ppermute x6, starting transfers between devices, extended(): lax.ppermute(lax.slice_in_dim(block, 0, width, axis=dim), axis, backward)  40.2 us
    gather x1, local copies, waits for them, and re-layouts, shards(): thrust_cell = jnp.where(inside, jnp.take(local_thrust(thrust), ids), 0.0)  24.7 us
    ppermute x6, starting transfers between devices, extended(): lax.ppermute(lax.slice_in_dim(block, block.shape[dim] - width, None, axis...  17.4 us
  transfers between devices with their start and end apart: 13, of which 6 were waited for; matrix products, arithmetic and copies ran while one was open for 8% of the time, Pallas kernels for 0%

profile of v1, /device:TPU:1, one launch (start us, length us, event | category | flops | bytes accessed | tf_op | source)
XLA Modules:
  0.0 394.6 jit_solution(1620338266631635886)
XLA Ops:
  7.2 1.0 fusion.1096
  8.2 5.4 %collective-permute-start = (f32[19,1,8,128]{3,2,1,0:T(8,128)S(1)}, f32[19,1,8,128]{3,2,1,0:T(8,128)S(1)}, u32[]{:S(2)}, u32[]{:S(2)}) collective-permute-start(f32[19,1,8,128]{3,2,1,0:T(8,128)S(1)} %get-tuple-element.327), channel_id=1, source_target_pairs={{0,8},{8,16},{16,24},{24,32},{32,40},{40,48},{48,56},{56,64},{64,7... | collective-permute-start | bytes 233480 | tf_op jit(solution)/shard_map/ppermute | solution.py:42
  13.6 5.4 %collective-permute-start.1 = (f32[19,1,8,128]{3,2,1,0:T(8,128)S(1)}, f32[19,1,8,128]{3,2,1,0:T(8,128)S(1)}, u32[]{:S(2)}, u32[]{:S(2)}) collective-permute-start(f32[19,1,8,128]{3,2,1,0:T(8,128)S(1)} %get-tuple-element.328), channel_id=1, source_target_pairs={{8,0},{16,8},{24,16},{32,24},{40,32},{48,40},{56,48},{64,56},{72,6... | collective-permute-start | bytes 233480 | tf_op jit(solution)/shard_map/ppermute | solution.py:45
  19.2 0.7 copy-done.8
  19.9 0.7 copy-done.7
  21.0 0.7 copy-done.10
  21.8 0.5 copy-done.11
  22.3 24.7 %gather_fusion = f32[4096]{0:T(1024)S(1)} fusion(f32[40]{0:T(128)S(1)} %multiply_divide_fusion, s32[4096]{0:T(1024)S(1)} %bitcast_clamp_fusion), kind=kCustom, calls=%fused_computation | custom fusion | bytes 49152 | tf_op jit(solution)/shard_map/jit(_take)/gather | solution.py:151
  47.2 1.9 collective-permute-start.2
  49.1 5.5 %collective-permute-start.3 = (f32[19,6,1,128]{3,2,1,0:T(1,128)S(1)}, f32[19,6,1,128]{3,2,1,0:T(1,128)S(1)}, u32[]{:S(2)}, u32[]{:S(2)}) collective-permute-start(f32[19,6,1,128]{3,2,1,0:T(1,128)S(1)} %get-tuple-element.264), channel_id=1, source_target_pairs={{1,0},{2,1},{3,2},{4,3},{5,4},{6,5},{7,6},{0,7},{9,8},{10,9},{11,1... | collective-permute-start | bytes 175112 | tf_op jit(solution)/shard_map/ppermute | solution.py:45
  54.8 1.1 collective-permute-done.3
  56.2 0.3 fusion.125
  56.6 0.4 broadcast_multiply_fusion.11
  57.0 0.3 divide_multiply_fusion.4
  57.4 0.3 multiply_bitcast_fusion.2
  57.7 0.5 fusion.668
  58.4 0.6 copy-done.9
  59.2 1.9 collective-permute-start.4
  61.1 9.9 %collective-permute-start.5 = (f32[19,1,8,128]{3,2,1,0:T(8,128)S(1)}, f32[19,1,8,128]{3,2,1,0:T(8,128)S(1)}, u32[]{:S(2)}, u32[]{:S(2)}) collective-permute-start(f32[19,1,8,128]{3,2,1,0:T(8,128)S(1)} %get-tuple-element.313), channel_id=1, source_target_pairs={{8,0},{16,8},{24,16},{32,24},{40,32},{48,40},{56,48},{64,56},{72,6... | collective-permute-start | bytes 233480 | tf_op jit(solution)/shard_map/ppermute | solution.py:45
  71.0 0.4 convolution_bitcast_fusion.2
  71.9 0.4 copy-done.3
  72.6 3.7 collective-permute-start.6
  76.3 4.3 %collective-permute-start.7 = (f32[19,6,1,128]{3,2,1,0:T(1,128)S(1)}, f32[19,6,1,128]{3,2,1,0:T(1,128)S(1)}, u32[]{:S(2)}, u32[]{:S(2)}) collective-permute-start(f32[19,6,1,128]{3,2,1,0:T(1,128)S(1)} %get-tuple-element.260), channel_id=1, source_target_pairs={{1,0},{2,1},{3,2},{4,3},{5,4},{6,5},{7,6},{0,7},{9,8},{10,9},{11,1... | collective-permute-start | bytes 175112 | tf_op jit(solution)/shard_map/ppermute | solution.py:45
  81.1 0.7 collective-permute-done.7
  82.2 0.3 add_add_fusion.54
  82.6 0.3 broadcast_multiply_fusion.13
  83.0 0.3 divide_multiply_fusion.2
  83.3 0.3 multiply_bitcast_fusion.1
  83.6 0.5 fusion.680
  84.3 0.5 pad_add_fusion.1
  84.9 1.9 collective-permute-start.8
  86.8 9.4 %collective-permute-start.9 = (f32[19,1,8,128]{3,2,1,0:T(8,128)S(1)}, f32[19,1,8,128]{3,2,1,0:T(8,128)S(1)}, u32[]{:S(2)}, u32[]{:S(2)}) collective-permute-start(f32[19,1,8,128]{3,2,1,0:T(8,128)S(1)} %get-tuple-element.299), channel_id=1, source_target_pairs={{8,0},{16,8},{24,16},{32,24},{40,32},{48,40},{56,48},{64,56},{72,6... | collective-permute-start | bytes 233480 | tf_op jit(solution)/shard_map/ppermute | solution.py:45
  96.2 0.4 convolution_bitcast_fusion.1
  97.1 0.4 copy-done.4
  97.8 2.5 collective-permute-start.10
  100.3 5.7 %collective-permute-start.11 = (f32[19,6,1,128]{3,2,1,0:T(1,128)S(1)}, f32[19,6,1,128]{3,2,1,0:T(1,128)S(1)}, u32[]{:S(2)}, u32[]{:S(2)}) collective-permute-start(f32[19,6,1,128]{3,2,1,0:T(1,128)S(1)} %get-tuple-element.256), channel_id=1, source_target_pairs={{1,0},{2,1},{3,2},{4,3},{5,4},{6,5},{7,6},{0,7},{9,8},{10,9},{11,1... | collective-permute-start | bytes 175112 | tf_op jit(solution)/shard_map/ppermute | solution.py:45
  106.5 0.6 collective-permute-done.11
  107.3 0.4 convolution_bitcast_fusion
  108.1 0.6 copy-done.2
  108.7 0.3 add_add_fusion.26
  109.2 0.3 broadcast_multiply_fusion.9
  109.5 0.3 divide_multiply_fusion
  110.1 0.5 fusion.692
  110.8 1.4 pad_add_fusion
  112.2 272.6 %all-reduce.264.cloned.1.call-done = (f32[20480]{0:T(1024)}, f32[20480]{0:T(1024)}, f32[20480]{0:T(1024)}) async-done(((f32[20480]{0:T(1024)}, f32[20480]{0:T(1024)}, f32[20480]{0:T(1024)}), (f32[20480]{0:T(1024)}, f32[20480]{0:T(1024)}, f32[20480]{0:T(1024)})) %all-reduce.264.cloned.1.call-update) | async-done | bytes 245776
  384.8 1.1 reshape.2493
  386.1 0.7 copy-done.5
  387.3 0.5 multiply_add_fusion.114
  (122 shorter events, 6.5 us)
Async XLA Ops:
  7.2 11.9 %copy-start = (f32[19,4,8,128]{3,2,1,0:T(8,128)S(1)}, f32[19,4,8,128]{3,2,1,0:T(8,128)}, u32[]{:S(2)}) copy-start(f32[19,4,8,128]{3,2,1,0:T(8,128)} %param.10) | copy-start | bytes 933892
  7.2 377.6 %all-reduce.264.cloned.1.call-start = ((), (), s32[]{:S(2)}) async-start(), calls=%async_computation | async-start | bytes 491520
  8.2 38.8 %collective-permute-start = (f32[19,1,8,128]{3,2,1,0:T(8,128)S(1)}, f32[19,1,8,128]{3,2,1,0:T(8,128)S(1)}, u32[]{:S(2)}, u32[]{:S(2)}) collective-permute-start(f32[19,1,8,128]{3,2,1,0:T(8,128)S(1)} %get-tuple-element.327), channel_id=1, source_target_pairs={{0,8},{8,16},{16,24},{24,32},{32,40},{40,48},{48,56},{56,64},{64,7... | collective-permute-start | bytes 233480 | tf_op jit(solution)/shard_map/ppermute | solution.py:42
  13.6 7.4 %copy-start.1 = (bf16[3,19,4,8,128]{4,3,2,1,0:T(8,128)(2,1)S(1)}, bf16[3,19,4,8,128]{4,3,2,1,0:T(8,128)(2,1)}, u32[]{:S(2)}) copy-start(bf16[3,19,4,8,128]{4,3,2,1,0:T(8,128)(2,1)} %param.8) | copy-start | bytes 1400836
  13.6 33.5 %collective-permute-start.1 = (f32[19,1,8,128]{3,2,1,0:T(8,128)S(1)}, f32[19,1,8,128]{3,2,1,0:T(8,128)S(1)}, u32[]{:S(2)}, u32[]{:S(2)}) collective-permute-start(f32[19,1,8,128]{3,2,1,0:T(8,128)S(1)} %get-tuple-element.328), channel_id=1, source_target_pairs={{8,0},{16,8},{24,16},{32,24},{40,32},{48,40},{56,48},{64,56},{72,6... | collective-permute-start | bytes 233480 | tf_op jit(solution)/shard_map/ppermute | solution.py:45
  19.1 0.8 copy-start.8
  19.9 0.7 copy-start.7
  20.9 0.7 copy-start.10
  21.6 0.7 copy-start.11
  47.2 7.6 %collective-permute-start.2 = (f32[19,6,1,128]{3,2,1,0:T(1,128)S(1)}, f32[19,6,1,128]{3,2,1,0:T(1,128)S(1)}, u32[]{:S(2)}, u32[]{:S(2)}) collective-permute-start(f32[19,6,1,128]{3,2,1,0:T(1,128)S(1)} %get-tuple-element.265), channel_id=1, source_target_pairs={{0,1},{1,2},{2,3},{3,4},{4,5},{5,6},{6,7},{7,0},{8,9},{9,10},{10,1... | collective-permute-start | bytes 175112 | tf_op jit(solution)/shard_map/ppermute | solution.py:42
  49.1 6.7 %collective-permute-start.3 = (f32[19,6,1,128]{3,2,1,0:T(1,128)S(1)}, f32[19,6,1,128]{3,2,1,0:T(1,128)S(1)}, u32[]{:S(2)}, u32[]{:S(2)}) collective-permute-start(f32[19,6,1,128]{3,2,1,0:T(1,128)S(1)} %get-tuple-element.264), channel_id=1, source_target_pairs={{1,0},{2,1},{3,2},{4,3},{5,4},{6,5},{7,6},{0,7},{9,8},{10,9},{11,1... | collective-permute-start | bytes 175112 | tf_op jit(solution)/shard_map/ppermute | solution.py:45
  58.4 0.7 copy-start.9
  59.2 12.5 %collective-permute-start.4 = (f32[19,1,8,128]{3,2,1,0:T(8,128)S(1)}, f32[19,1,8,128]{3,2,1,0:T(8,128)S(1)}, u32[]{:S(2)}, u32[]{:S(2)}) collective-permute-start(f32[19,1,8,128]{3,2,1,0:T(8,128)S(1)} %get-tuple-element.312), channel_id=1, source_target_pairs={{0,8},{8,16},{16,24},{24,32},{32,40},{40,48},{48,56},{56,64},{64,7... | collective-permute-start | bytes 233480 | tf_op jit(solution)/shard_map/ppermute | solution.py:42
  61.1 10.8 %collective-permute-start.5 = (f32[19,1,8,128]{3,2,1,0:T(8,128)S(1)}, f32[19,1,8,128]{3,2,1,0:T(8,128)S(1)}, u32[]{:S(2)}, u32[]{:S(2)}) collective-permute-start(f32[19,1,8,128]{3,2,1,0:T(8,128)S(1)} %get-tuple-element.313), channel_id=1, source_target_pairs={{8,0},{16,8},{24,16},{32,24},{40,32},{48,40},{56,48},{64,56},{72,6... | collective-permute-start | bytes 233480 | tf_op jit(solution)/shard_map/ppermute | solution.py:45
  71.7 0.6 copy-start.3
  72.6 8.5 %collective-permute-start.6 = (f32[19,6,1,128]{3,2,1,0:T(1,128)S(1)}, f32[19,6,1,128]{3,2,1,0:T(1,128)S(1)}, u32[]{:S(2)}, u32[]{:S(2)}) collective-permute-start(f32[19,6,1,128]{3,2,1,0:T(1,128)S(1)} %get-tuple-element.261), channel_id=1, source_target_pairs={{0,1},{1,2},{2,3},{3,4},{4,5},{5,6},{6,7},{7,0},{8,9},{9,10},{10,1... | collective-permute-start | bytes 175112 | tf_op jit(solution)/shard_map/ppermute | solution.py:42
  76.3 5.6 %collective-permute-start.7 = (f32[19,6,1,128]{3,2,1,0:T(1,128)S(1)}, f32[19,6,1,128]{3,2,1,0:T(1,128)S(1)}, u32[]{:S(2)}, u32[]{:S(2)}) collective-permute-start(f32[19,6,1,128]{3,2,1,0:T(1,128)S(1)} %get-tuple-element.260), channel_id=1, source_target_pairs={{1,0},{2,1},{3,2},{4,3},{5,4},{6,5},{7,6},{0,7},{9,8},{10,9},{11,1... | collective-permute-start | bytes 175112 | tf_op jit(solution)/shard_map/ppermute | solution.py:45
  84.9 12.1 %collective-permute-start.8 = (f32[19,1,8,128]{3,2,1,0:T(8,128)S(1)}, f32[19,1,8,128]{3,2,1,0:T(8,128)S(1)}, u32[]{:S(2)}, u32[]{:S(2)}) collective-permute-start(f32[19,1,8,128]{3,2,1,0:T(8,128)S(1)} %get-tuple-element.298), channel_id=1, source_target_pairs={{0,8},{8,16},{16,24},{24,32},{32,40},{40,48},{48,56},{56,64},{64,7... | collective-permute-start | bytes 233480 | tf_op jit(solution)/shard_map/ppermute | solution.py:42
  86.8 10.3 %collective-permute-start.9 = (f32[19,1,8,128]{3,2,1,0:T(8,128)S(1)}, f32[19,1,8,128]{3,2,1,0:T(8,128)S(1)}, u32[]{:S(2)}, u32[]{:S(2)}) collective-permute-start(f32[19,1,8,128]{3,2,1,0:T(8,128)S(1)} %get-tuple-element.299), channel_id=1, source_target_pairs={{8,0},{16,8},{24,16},{32,24},{40,32},{48,40},{56,48},{64,56},{72,6... | collective-permute-start | bytes 233480 | tf_op jit(solution)/shard_map/ppermute | solution.py:45
  96.9 0.6 copy-start.4
  97.8 8.7 %collective-permute-start.10 = (f32[19,6,1,128]{3,2,1,0:T(1,128)S(1)}, f32[19,6,1,128]{3,2,1,0:T(1,128)S(1)}, u32[]{:S(2)}, u32[]{:S(2)}) collective-permute-start(f32[19,6,1,128]{3,2,1,0:T(1,128)S(1)} %get-tuple-element.257), channel_id=1, source_target_pairs={{0,1},{1,2},{2,3},{3,4},{4,5},{5,6},{6,7},{7,0},{8,9},{9,10},{10,1... | collective-permute-start | bytes 175112 | tf_op jit(solution)/shard_map/ppermute | solution.py:42
  100.3 6.7 %collective-permute-start.11 = (f32[19,6,1,128]{3,2,1,0:T(1,128)S(1)}, f32[19,6,1,128]{3,2,1,0:T(1,128)S(1)}, u32[]{:S(2)}, u32[]{:S(2)}) collective-permute-start(f32[19,6,1,128]{3,2,1,0:T(1,128)S(1)} %get-tuple-element.256), channel_id=1, source_target_pairs={{1,0},{2,1},{3,2},{4,3},{5,4},{6,5},{7,6},{0,7},{9,8},{10,9},{11,1... | collective-permute-start | bytes 175112 | tf_op jit(solution)/shard_map/ppermute | solution.py:45
  108.1 0.6 copy-start.2
  384.8 1.1 copy-start.6
  385.9 0.9 copy-start.5
Sparse Core Ops, SparseCore 0:
  108.8 275.9 all-reduce.263
